TPU v7x, 32 devices: a whole 2x2x4 slice. The times are simulated.
32 devices in a mesh: rows: 8 (over y, x, core), blk: 4 (over z).
Axes of the slice: x: 2, y: 2, z: 4, core: 2. Of those that a mesh axis runs over, the one named last changes fastest.
Arguments:
- vectors: float32 [6144, 128], P('blk'), may hold values from -6 to 6
- left_intersection: float32 [256, 128, 128], P(('rows', 'blk')), may hold values from -0.5 to 0.5
- right_intersection: float32 [48, 128, 128], P('blk'), may hold values from -0.5 to 0.5
- tiles: float32 [512, 128, 128], P('rows'), may hold values from -0.09375 to 0.09375
- pair_cols: int32 [256, 32], P(('rows', 'blk')), may hold values from 0 to 47, all different within a row
- pair_owner: int32 [256, 32], P(('rows', 'blk')), may hold values from 0 to 7, as said below
- pair_slot: int32 [256, 32], P(('rows', 'blk')), may hold values from 0 to 63
- pair_counts: int32 [256], P(('rows', 'blk')), may hold values from 1 to 32, as said below
Outputs:
- product: float32 [32768, 128], P(('rows', 'blk'))
Inputs may be any that keep to these rules, and one draw needn't show every extreme that they name: `pair_owner`: among the 256 entries of each aligned block of 8 row blocks, every rows index appears exactly 32 times. `pair_cols`: the column blocks listed for one row block are distinct. `pair_counts`: some row block has all 32 entries live.
All inputs are finite; a program needn't handle non-finite values.
Results may differ from a plain program's by a relative error of at most 0.0003.
Values sent between devices are 32-bit elements; how exact they have to be, the bound alone decides.
No kernel may reach another device: no remote copies, remote signals or barrier semaphores. Data moves between devices by JAX's collectives and lax.ppermute only.
A program may use at most 128 MiB of HBM per device.

v0:
```python
import jax
import jax.numpy as jnp
from jax import lax
from jax.sharding import PartitionSpec as P


def pick_rows(table, row_ids, table_rows):
    onehot = (row_ids[:, None] == jnp.arange(table_rows)[None, :]).astype(jnp.float32)
    flat = table.reshape(table_rows, -1)
    picked = jnp.dot(
        onehot, flat, precision=lax.Precision.HIGHEST, preferred_element_type=jnp.float32
    )
    return picked.reshape((row_ids.shape[0],) + table.shape[1:])


def invert_slots(values, slot_index):
    count = slot_index.shape[0]
    matches = slot_index[None, :] == jnp.arange(count)[:, None]
    return jnp.sum(jnp.where(matches, values[None, :], 0), axis=1)


def per_device(
    vectors,
    left_intersection,
    right_intersection,
    tiles,
    pair_cols,
    pair_owner,
    pair_slot,
    pair_counts,
):
    row_blocks, fine_rows, coarse = left_intersection.shape
    listed = pair_cols.shape[1]
    vec_count = vectors.shape[1]
    owners = lax.axis_size("rows")
    entries = row_blocks * listed
    per_owner = entries // owners
    highest = lax.Precision.HIGHEST
    held_tiles = tiles.shape[0]
    flat_owner = pair_owner.reshape(entries)
    earlier = jnp.arange(entries)[:, None] > jnp.arange(entries)[None, :]
    matches = flat_owner[:, None] == flat_owner[None, :]
    position = jnp.sum(jnp.where(matches & earlier, 1, 0), axis=1).astype(jnp.int32)
    slot_index = flat_owner * per_owner + position
    local_blocks = vectors.reshape(right_intersection.shape[0], fine_rows, vec_count)
    entry_ids = jnp.arange(entries)
    block_ids = entry_ids // listed
    count_each = jnp.repeat(pair_counts, listed)
    live_flags = (entry_ids % listed < count_each).astype(jnp.int32)
    block_range = jnp.arange(row_blocks)
    slot_req = invert_slots(pair_slot.reshape(entries), slot_index)
    col_req = invert_slots(pair_cols.reshape(entries), slot_index)
    block_req = invert_slots(block_ids, slot_index)
    live_req = invert_slots(live_flags, slot_index)
    stacked = jnp.stack([slot_req, col_req, block_req, live_req]).reshape(4, owners, per_owner)
    received = lax.all_to_all(stacked, "rows", split_axis=1, concat_axis=1, tiled=True)
    local_proj = jnp.einsum("csu,csv->cuv", right_intersection, local_blocks, precision=highest)
    proj_all = lax.all_gather(local_proj, "blk", axis=0, tiled=True)
    col_total = proj_all.shape[0]

    def per_source(packed):
        slots_here, cols_here, blocks_here, live_here = packed
        chosen = pick_rows(tiles, slots_here, held_tiles)
        picked = pick_rows(proj_all, cols_here, col_total)
        applied = jnp.einsum("ptu,puv->ptv", chosen, picked, precision=highest)
        weights = (
            (blocks_here[None, :] == block_range[:, None]) & (live_here[None, :] > 0)
        ).astype(jnp.float32)
        return jnp.einsum("rp,ptv->rtv", weights, applied, precision=highest)

    partial_sums = lax.map(per_source, (received[0], received[1], received[2], received[3]))
    returned = lax.all_to_all(partial_sums, "rows", split_axis=0, concat_axis=0, tiled=True)
    summed = jnp.sum(returned, axis=0)
    result = jnp.einsum("bft,btv->bfv", left_intersection, summed, precision=highest)
    return result.reshape(row_blocks * fine_rows, vec_count)


def solution(mesh):
    return jax.shard_map(
        per_device,
        mesh=mesh,
        in_specs=(
            P("blk", None),
            P(("rows", "blk"), None, None),
            P("blk", None, None),
            P("rows", None, None),
            P(("rows", "blk"), None),
            P(("rows", "blk"), None),
            P(("rows", "blk"), None),
            P(("rows", "blk")),
        ),
        out_specs=P(("rows", "blk"), None),
        check_vma=False,
    )
```

profile of v0, /device:TPU:0, one launch (start us, length us, event | category | flops | bytes accessed | tf_op | source)
XLA Modules:
  0.0 277.5 jit_solution(6628994686971753800)
XLA Ops:
  7.7 3.4 %fusion.40 = f32[12,128,128]{2,1,0:T(8,128)} fusion(f32[12,128,128]{2,1,0:T(8,128)} %param.12, f32[12,128,128]{2,1,0:T(8,128)S(1)} %bitcast.91), kind=kOutput, calls=%fused_computation.57 | convolution fusion | flops 301989888 | bytes 2359296 | tf_op jit(solution)/shard_map/csu,csv->cuv/dot_general | solution.py:57
  13.0 5.2 %all-to-all-start = ((s32[8,1,128]{2,1,0:T(1,128)}), s32[8,1,128]{2,1,0:T(1,128)S(1)}, u32[]{:S(2)}, u32[]{:S(2)}) async-start(s32[8,1,128]{2,1,0:T(1,128)} %reshape.85), calls=%async_computation | async-start | bytes 8192 | tf_op jit(solution)/shard_map/all_to_all | solution.py:56
  18.2 4.6 %all-to-all-done = s32[8,1,128]{2,1,0:T(1,128)S(1)} async-done(((s32[8,1,128]{2,1,0:T(1,128)}), s32[8,1,128]{2,1,0:T(1,128)S(1)}, u32[]{:S(2)}, u32[]{:S(2)}) %all-to-all-start) | async-done | bytes 4128 | tf_op jit(solution)/shard_map/all_to_all | solution.py:56
  24.1 53.3 %all-gather.2.cloned.1.call-done = f32[48,128,128]{2,1,0:T(8,128)} async-done(((f32[12,128,128]{2,1,0:T(8,128)}), f32[48,128,128]{2,1,0:T(8,128)}) %all-gather.2.cloned.1.call-update) | async-done | bytes 3145744 | tf_op jit(solution)/shard_map/all_gather | solution.py:58
  77.5 135.7 %while.11 = (s32[]{:T(128)}, f32[8,8,128,128]{3,1,2,0:T(8,128)}, s32[8,32]{1,0:T(8,128)S(1)}, s32[8,32]{1,0:T(8,128)S(1)}, s32[8,32]{1,0:T(8,128)S(1)}, /*index=...) while((s32[]{:T(128)}, f32[8,8,128,128]{3,1,2,0:T(8,128)}, ...), condition=%wide.region_6.7_spmd.clone, body=%wide.region_5.6_spmd.clone.sunk | while | flops 1560285184 | bytes 33032132 | solution.py:71
  77.5 6.2 %fusion.69 = f32[32,128,128]{2,0,1:T(8,128)S(1)} fusion(s32[32]{0:T(128)S(1)} %get-tuple-element.150, f32[8,8,128,128]{3,2,1,0:T(8,128)} %bitcast.92), kind=kOutput, calls=%fused_computation.2.clone.1 | convolution fusion | flops 402655232 | bytes 6291584 | tf_op jit(solution)/shard_map/while/body/eval_jaxpr/dot_general | solution.py:10
  83.7 3.3 %fusion.67 = f32[32,128,128]{2,0,1:T(8,128)S(1)} fusion(s32[32]{0:T(128)S(1)} %fusion.66, f32[6,8,128,128]{3,2,1,0:T(8,128)S(1)} %bitcast.93), kind=kOutput, calls=%fused_computation.6.clone.1 | convolution fusion | flops 301991424 | bytes 5243008 | tf_op jit(solution)/shard_map/while/body/eval_jaxpr/dot_general | solution.py:10
  87.0 4.6 %fusion.70 = f32[32,128,128]{2,1,0:T(8,128)S(1)} fusion(f32[32,128,128]{2,0,1:T(8,128)S(1)} %fusion.67, f32[32,128,128]{2,0,1:T(8,128)S(1)} %fusion.69), kind=kOutput, calls=%fused_computation.11.clone.1 | convolution fusion | flops 805306368 | bytes 6291456 | tf_op jit(solution)/shard_map/while/body/eval_jaxpr/ptu,puv->ptv/dot_general | solution.py:65
  94.4 6.2 %fusion.69 = f32[32,128,128]{2,0,1:T(8,128)S(1)} fusion(s32[32]{0:T(128)S(1)} %get-tuple-element.150, f32[8,8,128,128]{3,2,1,0:T(8,128)} %bitcast.92), kind=kOutput, calls=%fused_computation.2.clone.1 | convolution fusion | flops 402655232 | bytes 6291584 | tf_op jit(solution)/shard_map/while/body/eval_jaxpr/dot_general | solution.py:10
  100.6 3.3 %fusion.67 = f32[32,128,128]{2,0,1:T(8,128)S(1)} fusion(s32[32]{0:T(128)S(1)} %fusion.66, f32[6,8,128,128]{3,2,1,0:T(8,128)S(1)} %bitcast.93), kind=kOutput, calls=%fused_computation.6.clone.1 | convolution fusion | flops 301991424 | bytes 5243008 | tf_op jit(solution)/shard_map/while/body/eval_jaxpr/dot_general | solution.py:10
  104.0 4.6 %fusion.70 = f32[32,128,128]{2,1,0:T(8,128)S(1)} fusion(f32[32,128,128]{2,0,1:T(8,128)S(1)} %fusion.67, f32[32,128,128]{2,0,1:T(8,128)S(1)} %fusion.69), kind=kOutput, calls=%fused_computation.11.clone.1 | convolution fusion | flops 805306368 | bytes 6291456 | tf_op jit(solution)/shard_map/while/body/eval_jaxpr/ptu,puv->ptv/dot_general | solution.py:65
  111.4 6.2 %fusion.69 = f32[32,128,128]{2,0,1:T(8,128)S(1)} fusion(s32[32]{0:T(128)S(1)} %get-tuple-element.150, f32[8,8,128,128]{3,2,1,0:T(8,128)} %bitcast.92), kind=kOutput, calls=%fused_computation.2.clone.1 | convolution fusion | flops 402655232 | bytes 6291584 | tf_op jit(solution)/shard_map/while/body/eval_jaxpr/dot_general | solution.py:10
  117.6 3.3 %fusion.67 = f32[32,128,128]{2,0,1:T(8,128)S(1)} fusion(s32[32]{0:T(128)S(1)} %fusion.66, f32[6,8,128,128]{3,2,1,0:T(8,128)S(1)} %bitcast.93), kind=kOutput, calls=%fused_computation.6.clone.1 | convolution fusion | flops 301991424 | bytes 5243008 | tf_op jit(solution)/shard_map/while/body/eval_jaxpr/dot_general | solution.py:10
  120.9 4.6 %fusion.70 = f32[32,128,128]{2,1,0:T(8,128)S(1)} fusion(f32[32,128,128]{2,0,1:T(8,128)S(1)} %fusion.67, f32[32,128,128]{2,0,1:T(8,128)S(1)} %fusion.69), kind=kOutput, calls=%fused_computation.11.clone.1 | convolution fusion | flops 805306368 | bytes 6291456 | tf_op jit(solution)/shard_map/while/body/eval_jaxpr/ptu,puv->ptv/dot_general | solution.py:65
  125.5 2.8 %fusion.71 = f32[8,8,128,128]{3,1,2,0:T(8,128)} fusion(f32[8,8,128,128]{3,1,2,0:T(8,128)} %get-tuple-element.162, s32[]{:T(128)} %get-tuple-element.161, f32[32,128,128]{2,1,0:T(8,128)S(1)} %fusion.70, s32[32]{0:T(128)S(1)} %get-tuple-element.151, pred[32]{0:T(512)(128)(4,1)S(1)} %compare_bitcast_fusion.2), kind=kOutput, calls=%fused_computation.15.clone.1 | convolution fusion | flops 50332160 | bytes 2622112 | tf_op jit(solution)/shard_map/while/body/eval_jaxpr/rp,ptv->rtv/dot_general | solution.py:69
  128.3 6.2 %fusion.69 = f32[32,128,128]{2,0,1:T(8,128)S(1)} fusion(s32[32]{0:T(128)S(1)} %get-tuple-element.150, f32[8,8,128,128]{3,2,1,0:T(8,128)} %bitcast.92), kind=kOutput, calls=%fused_computation.2.clone.1 | convolution fusion | flops 402655232 | bytes 6291584 | tf_op jit(solution)/shard_map/while/body/eval_jaxpr/dot_general | solution.py:10
  134.6 3.3 %fusion.67 = f32[32,128,128]{2,0,1:T(8,128)S(1)} fusion(s32[32]{0:T(128)S(1)} %fusion.66, f32[6,8,128,128]{3,2,1,0:T(8,128)S(1)} %bitcast.93), kind=kOutput, calls=%fused_computation.6.clone.1 | convolution fusion | flops 301991424 | bytes 5243008 | tf_op jit(solution)/shard_map/while/body/eval_jaxpr/dot_general | solution.py:10
  137.9 4.6 %fusion.70 = f32[32,128,128]{2,1,0:T(8,128)S(1)} fusion(f32[32,128,128]{2,0,1:T(8,128)S(1)} %fusion.67, f32[32,128,128]{2,0,1:T(8,128)S(1)} %fusion.69), kind=kOutput, calls=%fused_computation.11.clone.1 | convolution fusion | flops 805306368 | bytes 6291456 | tf_op jit(solution)/shard_map/while/body/eval_jaxpr/ptu,puv->ptv/dot_general | solution.py:65
  145.3 6.2 %fusion.69 = f32[32,128,128]{2,0,1:T(8,128)S(1)} fusion(s32[32]{0:T(128)S(1)} %get-tuple-element.150, f32[8,8,128,128]{3,2,1,0:T(8,128)} %bitcast.92), kind=kOutput, calls=%fused_computation.2.clone.1 | convolution fusion | flops 402655232 | bytes 6291584 | tf_op jit(solution)/shard_map/while/body/eval_jaxpr/dot_general | solution.py:10
  151.5 3.3 %fusion.67 = f32[32,128,128]{2,0,1:T(8,128)S(1)} fusion(s32[32]{0:T(128)S(1)} %fusion.66, f32[6,8,128,128]{3,2,1,0:T(8,128)S(1)} %bitcast.93), kind=kOutput, calls=%fused_computation.6.clone.1 | convolution fusion | flops 301991424 | bytes 5243008 | tf_op jit(solution)/shard_map/while/body/eval_jaxpr/dot_general | solution.py:10
  154.9 4.6 %fusion.70 = f32[32,128,128]{2,1,0:T(8,128)S(1)} fusion(f32[32,128,128]{2,0,1:T(8,128)S(1)} %fusion.67, f32[32,128,128]{2,0,1:T(8,128)S(1)} %fusion.69), kind=kOutput, calls=%fused_computation.11.clone.1 | convolution fusion | flops 805306368 | bytes 6291456 | tf_op jit(solution)/shard_map/while/body/eval_jaxpr/ptu,puv->ptv/dot_general | solution.py:65
  162.2 6.2 %fusion.69 = f32[32,128,128]{2,0,1:T(8,128)S(1)} fusion(s32[32]{0:T(128)S(1)} %get-tuple-element.150, f32[8,8,128,128]{3,2,1,0:T(8,128)} %bitcast.92), kind=kOutput, calls=%fused_computation.2.clone.1 | convolution fusion | flops 402655232 | bytes 6291584 | tf_op jit(solution)/shard_map/while/body/eval_jaxpr/dot_general | solution.py:10
  168.5 3.3 %fusion.67 = f32[32,128,128]{2,0,1:T(8,128)S(1)} fusion(s32[32]{0:T(128)S(1)} %fusion.66, f32[6,8,128,128]{3,2,1,0:T(8,128)S(1)} %bitcast.93), kind=kOutput, calls=%fused_computation.6.clone.1 | convolution fusion | flops 301991424 | bytes 5243008 | tf_op jit(solution)/shard_map/while/body/eval_jaxpr/dot_general | solution.py:10
  171.8 4.6 %fusion.70 = f32[32,128,128]{2,1,0:T(8,128)S(1)} fusion(f32[32,128,128]{2,0,1:T(8,128)S(1)} %fusion.67, f32[32,128,128]{2,0,1:T(8,128)S(1)} %fusion.69), kind=kOutput, calls=%fused_computation.11.clone.1 | convolution fusion | flops 805306368 | bytes 6291456 | tf_op jit(solution)/shard_map/while/body/eval_jaxpr/ptu,puv->ptv/dot_general | solution.py:65
  179.2 6.2 %fusion.69 = f32[32,128,128]{2,0,1:T(8,128)S(1)} fusion(s32[32]{0:T(128)S(1)} %get-tuple-element.150, f32[8,8,128,128]{3,2,1,0:T(8,128)} %bitcast.92), kind=kOutput, calls=%fused_computation.2.clone.1 | convolution fusion | flops 402655232 | bytes 6291584 | tf_op jit(solution)/shard_map/while/body/eval_jaxpr/dot_general | solution.py:10
  185.5 3.3 %fusion.67 = f32[32,128,128]{2,0,1:T(8,128)S(1)} fusion(s32[32]{0:T(128)S(1)} %fusion.66, f32[6,8,128,128]{3,2,1,0:T(8,128)S(1)} %bitcast.93), kind=kOutput, calls=%fused_computation.6.clone.1 | convolution fusion | flops 301991424 | bytes 5243008 | tf_op jit(solution)/shard_map/while/body/eval_jaxpr/dot_general | solution.py:10
  188.8 4.6 %fusion.70 = f32[32,128,128]{2,1,0:T(8,128)S(1)} fusion(f32[32,128,128]{2,0,1:T(8,128)S(1)} %fusion.67, f32[32,128,128]{2,0,1:T(8,128)S(1)} %fusion.69), kind=kOutput, calls=%fused_computation.11.clone.1 | convolution fusion | flops 805306368 | bytes 6291456 | tf_op jit(solution)/shard_map/while/body/eval_jaxpr/ptu,puv->ptv/dot_general | solution.py:65
  196.1 6.2 %fusion.69 = f32[32,128,128]{2,0,1:T(8,128)S(1)} fusion(s32[32]{0:T(128)S(1)} %get-tuple-element.150, f32[8,8,128,128]{3,2,1,0:T(8,128)} %bitcast.92), kind=kOutput, calls=%fused_computation.2.clone.1 | convolution fusion | flops 402655232 | bytes 6291584 | tf_op jit(solution)/shard_map/while/body/eval_jaxpr/dot_general | solution.py:10
  202.4 3.3 %fusion.67 = f32[32,128,128]{2,0,1:T(8,128)S(1)} fusion(s32[32]{0:T(128)S(1)} %fusion.66, f32[6,8,128,128]{3,2,1,0:T(8,128)S(1)} %bitcast.93), kind=kOutput, calls=%fused_computation.6.clone.1 | convolution fusion | flops 301991424 | bytes 5243008 | tf_op jit(solution)/shard_map/while/body/eval_jaxpr/dot_general | solution.py:10
  205.7 4.6 %fusion.70 = f32[32,128,128]{2,1,0:T(8,128)S(1)} fusion(f32[32,128,128]{2,0,1:T(8,128)S(1)} %fusion.67, f32[32,128,128]{2,0,1:T(8,128)S(1)} %fusion.69), kind=kOutput, calls=%fused_computation.11.clone.1 | convolution fusion | flops 805306368 | bytes 6291456 | tf_op jit(solution)/shard_map/while/body/eval_jaxpr/ptu,puv->ptv/dot_general | solution.py:65
  210.3 2.8 %fusion.71 = f32[8,8,128,128]{3,1,2,0:T(8,128)} fusion(f32[8,8,128,128]{3,1,2,0:T(8,128)} %get-tuple-element.162, s32[]{:T(128)} %get-tuple-element.161, f32[32,128,128]{2,1,0:T(8,128)S(1)} %fusion.70, s32[32]{0:T(128)S(1)} %get-tuple-element.151, pred[32]{0:T(512)(128)(4,1)S(1)} %compare_bitcast_fusion.2), kind=kOutput, calls=%fused_computation.15.clone.1 | convolution fusion | flops 50332160 | bytes 2622112 | tf_op jit(solution)/shard_map/while/body/eval_jaxpr/rp,ptv->rtv/dot_general | solution.py:69
  213.1 53.5 %all_to_all.10 = f32[8,8,128,128]{3,1,2,0:T(8,128)} all-to-all(f32[8,8,128,128]{3,1,2,0:T(8,128)} %get-tuple-element.52), channel_id=1, replica_groups=mesh['rows'=8,'blk'=4] {'rows'}, dimensions={0} | all-to-all | bytes 8388608 | tf_op jit(solution)/shard_map/all_to_all | solution.py:72
  (82 shorter events, 25.1 us)
Async XLA Ops:
  6.5 1.1 copy-start
  6.5 4.6 %copy-start.3 = (s32[8,32]{1,0:T(8,128)S(1)}, s32[8,32]{1,0:T(8,128)}, u32[]{:S(2)}) copy-start(s32[8,32]{1,0:T(8,128)} %param.15) | copy-start | bytes 3076
  6.5 4.7 %copy-start.6 = (s32[8]{0:T(128)S(1)}, s32[8]{0:T(128)}, u32[]{:S(2)}) copy-start(s32[8]{0:T(128)} %param.17) | copy-start | bytes 100
  6.5 4.8 %copy-start.4 = (s32[8,32]{1,0:T(8,128)S(1)}, s32[8,32]{1,0:T(8,128)}, u32[]{:S(2)}) copy-start(s32[8,32]{1,0:T(8,128)} %param.16) | copy-start | bytes 3076
  6.5 4.9 %copy-start.5 = (s32[8,32]{1,0:T(8,128)S(1)}, s32[8,32]{1,0:T(8,128)}, u32[]{:S(2)}) copy-start(s32[8,32]{1,0:T(8,128)} %param.14) | copy-start | bytes 3076
  6.5 70.9 %all-gather.2.cloned.1.call-start = ((), (), s32[]{:S(2)}) async-start(), calls=%async_computation.2 | async-start | bytes 3932160 | tf_op jit(solution)/shard_map/all_gather | solution.py:58
  13.0 9.8 %all-to-all-start = ((s32[8,1,128]{2,1,0:T(1,128)}), s32[8,1,128]{2,1,0:T(1,128)S(1)}, u32[]{:S(2)}, u32[]{:S(2)}) async-start(s32[8,1,128]{2,1,0:T(1,128)} %reshape.85), calls=%async_computation | async-start | bytes 8192 | tf_op jit(solution)/shard_map/all_to_all | solution.py:56
  77.5 6.2 %copy-start.1 = (f32[48,128,128]{2,1,0:T(8,128)S(1)}, f32[48,128,128]{2,1,0:T(8,128)}, u32[]{:S(2)}) copy-start(f32[48,128,128]{2,1,0:T(8,128)} %get-tuple-element.177) | copy-start | bytes 9437188 | tf_op jit(solution)/shard_map/while
  94.4 6.2 %copy-start.1 = (f32[48,128,128]{2,1,0:T(8,128)S(1)}, f32[48,128,128]{2,1,0:T(8,128)}, u32[]{:S(2)}) copy-start(f32[48,128,128]{2,1,0:T(8,128)} %get-tuple-element.177) | copy-start | bytes 9437188 | tf_op jit(solution)/shard_map/while
  111.4 6.2 %copy-start.1 = (f32[48,128,128]{2,1,0:T(8,128)S(1)}, f32[48,128,128]{2,1,0:T(8,128)}, u32[]{:S(2)}) copy-start(f32[48,128,128]{2,1,0:T(8,128)} %get-tuple-element.177) | copy-start | bytes 9437188 | tf_op jit(solution)/shard_map/while
  128.3 6.2 %copy-start.1 = (f32[48,128,128]{2,1,0:T(8,128)S(1)}, f32[48,128,128]{2,1,0:T(8,128)}, u32[]{:S(2)}) copy-start(f32[48,128,128]{2,1,0:T(8,128)} %get-tuple-element.177) | copy-start | bytes 9437188 | tf_op jit(solution)/shard_map/while
  145.3 6.2 %copy-start.1 = (f32[48,128,128]{2,1,0:T(8,128)S(1)}, f32[48,128,128]{2,1,0:T(8,128)}, u32[]{:S(2)}) copy-start(f32[48,128,128]{2,1,0:T(8,128)} %get-tuple-element.177) | copy-start | bytes 9437188 | tf_op jit(solution)/shard_map/while
  162.2 6.2 %copy-start.1 = (f32[48,128,128]{2,1,0:T(8,128)S(1)}, f32[48,128,128]{2,1,0:T(8,128)}, u32[]{:S(2)}) copy-start(f32[48,128,128]{2,1,0:T(8,128)} %get-tuple-element.177) | copy-start | bytes 9437188 | tf_op jit(solution)/shard_map/while
  179.2 6.2 %copy-start.1 = (f32[48,128,128]{2,1,0:T(8,128)S(1)}, f32[48,128,128]{2,1,0:T(8,128)}, u32[]{:S(2)}) copy-start(f32[48,128,128]{2,1,0:T(8,128)} %get-tuple-element.177) | copy-start | bytes 9437188 | tf_op jit(solution)/shard_map/while
  196.1 6.2 %copy-start.1 = (f32[48,128,128]{2,1,0:T(8,128)S(1)}, f32[48,128,128]{2,1,0:T(8,128)}, u32[]{:S(2)}) copy-start(f32[48,128,128]{2,1,0:T(8,128)} %get-tuple-element.177) | copy-start | bytes 9437188 | tf_op jit(solution)/shard_map/while
  266.6 2.5 copy-start.2
Sparse Core Ops, SparseCore 0:
  11.2 66.1 all-gather.1
where the time goes:
time: 278 us; the launch traced here: 277 us
  matrix products  140 us (50%)
  waiting for transfers between devices  58 us (21%)
  blocking collectives  53.5 us (19%)
  between operations  13.5 us (5%)
  starting transfers between devices  5.24 us (2%)
  other arithmetic  3.71 us (1%)
  local copies, waits for them, and re-layouts  3.25 us (1%)
    dot_general x16, matrix products, pick_rows(): jnp.dot(onehot, flat, precision=lax.Precision.HIGHEST, preferred_element_...  76.3 us
    all_to_all x1, blocking collectives, per_device(): lax.all_to_all(partial_sums, 'rows', split_axis=0, concat_axis=0, tiled=T...  53.5 us
    all_gather x1, waiting for transfers between devices, per_device(): proj_all = lax.all_gather(local_proj, 'blk', axis=0, tiled=True)  53.3 us
    dot_general x8, matrix products, per_source(): applied = jnp.einsum('ptu,puv->ptv', chosen, picked, precision=highest)  36.6 us
    dot_general x8, matrix products, per_source(): return jnp.einsum('rp,ptv->rtv', weights, applied, precision=highest)  22.2 us
  transfers between devices with their start and end apart: 2, of which 2 were waited for; matrix products, arithmetic and copies ran while one was open for 1% of the time, Pallas kernels for 0%

commit v1 on v0

--- a/solution.py
+++ b/solution.py
@@ -2,6 +2,17 @@
 import jax.numpy as jnp
 from jax import lax
 from jax.sharding import PartitionSpec as P
+
+
+def in_blocks(array, dim, size):
+    before, after = (array.shape[:dim], array.shape[dim + 1 :])
+    return jnp.moveaxis(array.reshape(*before, size, -1, *after), dim, 0)
+
+
+def joined_along(blocks, dim):
+    blocks = jnp.moveaxis(blocks, 0, dim)
+    lengths = blocks.shape
+    return blocks.reshape(*lengths[:dim], lengths[dim] * lengths[dim + 1], *lengths[dim + 2 :])
 
 
 def pick_rows(table, row_ids, table_rows):
@@ -53,7 +64,14 @@
     block_req = invert_slots(block_ids, slot_index)
     live_req = invert_slots(live_flags, slot_index)
     stacked = jnp.stack([slot_req, col_req, block_req, live_req]).reshape(4, owners, per_owner)
-    received = lax.all_to_all(stacked, "rows", split_axis=1, concat_axis=1, tiled=True)
+    devices, index = (lax.axis_size("rows"), lax.axis_index("rows"))
+    pieces = in_blocks(stacked, 1, devices)
+    finished = [pieces[index]]
+    for step in range(1, devices):
+        sent = pieces[index ^ step]
+        finished.append(lax.ppermute(sent, "rows", [(i, i ^ step) for i in range(devices)]))
+    pieces = jnp.stack(finished)[index ^ jnp.arange(devices)]
+    received = joined_along(pieces, 1)
     local_proj = jnp.einsum("csu,csv->cuv", right_intersection, local_blocks, precision=highest)
     proj_all = lax.all_gather(local_proj, "blk", axis=0, tiled=True)
     col_total = proj_all.shape[0]

time: 278 us -> 278 us (level)
    ppermute x0 -> x7, starting transfers between devices: none -> 7.75 us  [per_device(): lax.ppermute(sent, 'rows', [(i, i ^ step) for i in range(devices)])]
    all_to_all x1 -> x0, starting transfers between devices: 5.2 us -> none  [per_device(): lax.all_to_all(stacked, 'rows', split_axis=1, concat_axis=1, tiled=True)]
    all_to_all x1 -> x0, waiting for transfers between devices: 4.61 us -> none  [per_device(): lax.all_to_all(stacked, 'rows', split_axis=1, concat_axis=1, tiled=True)]
    ppermute x0 -> x7, waiting for transfers between devices: none -> 3.74 us  [per_device(): lax.ppermute(sent, 'rows', [(i, i ^ step) for i in range(devices)])]
  transfers between devices with their start and end apart: 2 -> 8, of which waited for: 2 -> 4; matrix products, arithmetic and copies ran while one was open for 1% -> 1% of each run, Pallas kernels for 0% -> 0%
where the time goes in v1:
time: 278 us; the launch traced here: 277 us
  matrix products  140 us (50%)
  waiting for transfers between devices  56.6 us (20%)
  blocking collectives  53.5 us (19%)
  between operations  13.5 us (5%)
  starting transfers between devices  7.79 us (3%)
  other arithmetic  3.07 us (1%)
    dot_general x16, matrix products, pick_rows(): jnp.dot(onehot, flat, precision=lax.Precision.HIGHEST, preferred_element_...  76.3 us
    all_to_all x1, blocking collectives, per_device(): lax.all_to_all(partial_sums, 'rows', split_axis=0, concat_axis=0, tiled=T...  53.5 us
    all_gather x1, waiting for transfers between devices, per_device(): proj_all = lax.all_gather(local_proj, 'blk', axis=0, tiled=True)  52.8 us
    dot_general x8, matrix products, per_source(): applied = jnp.einsum('ptu,puv->ptv', chosen, picked, precision=highest)  36.6 us
    dot_general x8, matrix products, per_source(): return jnp.einsum('rp,ptv->rtv', weights, applied, precision=highest)  22.1 us
    ppermute x7, starting transfers between devices, per_device(): lax.ppermute(sent, 'rows', [(i, i ^ step) for i in range(devices)])  7.75 us
  transfers between devices with their start and end apart: 8, of which 4 were waited for; matrix products, arithmetic and copies ran while one was open for 1% of the time, Pallas kernels for 0%

profile of v1, /device:TPU:0, one launch (start us, length us, event | category | flops | bytes accessed | tf_op | source)
XLA Modules:
  0.0 277.4 jit_solution(7954333062043693140)
XLA Ops:
  7.7 3.5 %fusion.40 = f32[12,128,128]{2,1,0:T(8,128)} fusion(f32[12,128,128]{2,1,0:T(8,128)} %param.12, f32[12,128,128]{2,1,0:T(8,128)S(1)} %bitcast.124), kind=kOutput, calls=%fused_computation.75 | convolution fusion | flops 301989888 | bytes 2359296 | tf_op jit(solution)/shard_map/csu,csv->cuv/dot_general | solution.py:75
  24.6 52.8 %all-gather.2.cloned.1.call-done = f32[48,128,128]{2,1,0:T(8,128)} async-done(((f32[12,128,128]{2,1,0:T(8,128)}), f32[48,128,128]{2,1,0:T(8,128)}) %all-gather.2.cloned.1.call-update) | async-done | bytes 3145744 | tf_op jit(solution)/shard_map/all_gather | solution.py:76
  77.5 135.6 %while.11 = (s32[]{:T(128)}, f32[8,8,128,128]{3,1,2,0:T(8,128)}, s32[8,32]{1,0:T(8,128)S(1)}, s32[8,32]{1,0:T(8,128)S(1)}, s32[8,32]{1,0:T(8,128)S(1)}, /*index=...) while((s32[]{:T(128)}, f32[8,8,128,128]{3,1,2,0:T(8,128)}, ...), condition=%wide.region_6.7_spmd.clone, body=%wide.region_5.6_spmd.clone.sunk | while | flops 1560285184 | bytes 33032132 | solution.py:89
  77.5 6.2 %fusion.69 = f32[32,128,128]{2,0,1:T(8,128)S(1)} fusion(s32[32]{0:T(128)S(1)} %get-tuple-element.157, f32[8,8,128,128]{3,2,1,0:T(8,128)} %bitcast.125), kind=kOutput, calls=%fused_computation.3.clone.1 | convolution fusion | flops 402655232 | bytes 6291584 | tf_op jit(solution)/shard_map/while/body/eval_jaxpr/dot_general | solution.py:21
  83.7 3.3 %fusion.67 = f32[32,128,128]{2,0,1:T(8,128)S(1)} fusion(s32[32]{0:T(128)S(1)} %fusion.66, f32[6,8,128,128]{3,2,1,0:T(8,128)S(1)} %bitcast.126), kind=kOutput, calls=%fused_computation.7.clone.1 | convolution fusion | flops 301991424 | bytes 5243008 | tf_op jit(solution)/shard_map/while/body/eval_jaxpr/dot_general | solution.py:21
  87.1 4.6 %fusion.70 = f32[32,128,128]{2,1,0:T(8,128)S(1)} fusion(f32[32,128,128]{2,0,1:T(8,128)S(1)} %fusion.67, f32[32,128,128]{2,0,1:T(8,128)S(1)} %fusion.69), kind=kOutput, calls=%fused_computation.12.clone.1 | convolution fusion | flops 805306368 | bytes 6291456 | tf_op jit(solution)/shard_map/while/body/eval_jaxpr/ptu,puv->ptv/dot_general | solution.py:83
  94.4 6.2 %fusion.69 = f32[32,128,128]{2,0,1:T(8,128)S(1)} fusion(s32[32]{0:T(128)S(1)} %get-tuple-element.157, f32[8,8,128,128]{3,2,1,0:T(8,128)} %bitcast.125), kind=kOutput, calls=%fused_computation.3.clone.1 | convolution fusion | flops 402655232 | bytes 6291584 | tf_op jit(solution)/shard_map/while/body/eval_jaxpr/dot_general | solution.py:21
  100.7 3.3 %fusion.67 = f32[32,128,128]{2,0,1:T(8,128)S(1)} fusion(s32[32]{0:T(128)S(1)} %fusion.66, f32[6,8,128,128]{3,2,1,0:T(8,128)S(1)} %bitcast.126), kind=kOutput, calls=%fused_computation.7.clone.1 | convolution fusion | flops 301991424 | bytes 5243008 | tf_op jit(solution)/shard_map/while/body/eval_jaxpr/dot_general | solution.py:21
  104.0 4.6 %fusion.70 = f32[32,128,128]{2,1,0:T(8,128)S(1)} fusion(f32[32,128,128]{2,0,1:T(8,128)S(1)} %fusion.67, f32[32,128,128]{2,0,1:T(8,128)S(1)} %fusion.69), kind=kOutput, calls=%fused_computation.12.clone.1 | convolution fusion | flops 805306368 | bytes 6291456 | tf_op jit(solution)/shard_map/while/body/eval_jaxpr/ptu,puv->ptv/dot_general | solution.py:83
  111.4 6.2 %fusion.69 = f32[32,128,128]{2,0,1:T(8,128)S(1)} fusion(s32[32]{0:T(128)S(1)} %get-tuple-element.157, f32[8,8,128,128]{3,2,1,0:T(8,128)} %bitcast.125), kind=kOutput, calls=%fused_computation.3.clone.1 | convolution fusion | flops 402655232 | bytes 6291584 | tf_op jit(solution)/shard_map/while/body/eval_jaxpr/dot_general | solution.py:21
  117.6 3.3 %fusion.67 = f32[32,128,128]{2,0,1:T(8,128)S(1)} fusion(s32[32]{0:T(128)S(1)} %fusion.66, f32[6,8,128,128]{3,2,1,0:T(8,128)S(1)} %bitcast.126), kind=kOutput, calls=%fused_computation.7.clone.1 | convolution fusion | flops 301991424 | bytes 5243008 | tf_op jit(solution)/shard_map/while/body/eval_jaxpr/dot_general | solution.py:21
  120.9 4.6 %fusion.70 = f32[32,128,128]{2,1,0:T(8,128)S(1)} fusion(f32[32,128,128]{2,0,1:T(8,128)S(1)} %fusion.67, f32[32,128,128]{2,0,1:T(8,128)S(1)} %fusion.69), kind=kOutput, calls=%fused_computation.12.clone.1 | convolution fusion | flops 805306368 | bytes 6291456 | tf_op jit(solution)/shard_map/while/body/eval_jaxpr/ptu,puv->ptv/dot_general | solution.py:83
  125.5 2.8 fusion.71
  128.3 6.2 %fusion.69 = f32[32,128,128]{2,0,1:T(8,128)S(1)} fusion(s32[32]{0:T(128)S(1)} %get-tuple-element.157, f32[8,8,128,128]{3,2,1,0:T(8,128)} %bitcast.125), kind=kOutput, calls=%fused_computation.3.clone.1 | convolution fusion | flops 402655232 | bytes 6291584 | tf_op jit(solution)/shard_map/while/body/eval_jaxpr/dot_general | solution.py:21
  134.6 3.3 %fusion.67 = f32[32,128,128]{2,0,1:T(8,128)S(1)} fusion(s32[32]{0:T(128)S(1)} %fusion.66, f32[6,8,128,128]{3,2,1,0:T(8,128)S(1)} %bitcast.126), kind=kOutput, calls=%fused_computation.7.clone.1 | convolution fusion | flops 301991424 | bytes 5243008 | tf_op jit(solution)/shard_map/while/body/eval_jaxpr/dot_general | solution.py:21
  137.9 4.6 %fusion.70 = f32[32,128,128]{2,1,0:T(8,128)S(1)} fusion(f32[32,128,128]{2,0,1:T(8,128)S(1)} %fusion.67, f32[32,128,128]{2,0,1:T(8,128)S(1)} %fusion.69), kind=kOutput, calls=%fused_computation.12.clone.1 | convolution fusion | flops 805306368 | bytes 6291456 | tf_op jit(solution)/shard_map/while/body/eval_jaxpr/ptu,puv->ptv/dot_general | solution.py:83
  145.3 6.2 %fusion.69 = f32[32,128,128]{2,0,1:T(8,128)S(1)} fusion(s32[32]{0:T(128)S(1)} %get-tuple-element.157, f32[8,8,128,128]{3,2,1,0:T(8,128)} %bitcast.125), kind=kOutput, calls=%fused_computation.3.clone.1 | convolution fusion | flops 402655232 | bytes 6291584 | tf_op jit(solution)/shard_map/while/body/eval_jaxpr/dot_general | solution.py:21
  151.5 3.3 %fusion.67 = f32[32,128,128]{2,0,1:T(8,128)S(1)} fusion(s32[32]{0:T(128)S(1)} %fusion.66, f32[6,8,128,128]{3,2,1,0:T(8,128)S(1)} %bitcast.126), kind=kOutput, calls=%fused_computation.7.clone.1 | convolution fusion | flops 301991424 | bytes 5243008 | tf_op jit(solution)/shard_map/while/body/eval_jaxpr/dot_general | solution.py:21
  154.8 4.6 %fusion.70 = f32[32,128,128]{2,1,0:T(8,128)S(1)} fusion(f32[32,128,128]{2,0,1:T(8,128)S(1)} %fusion.67, f32[32,128,128]{2,0,1:T(8,128)S(1)} %fusion.69), kind=kOutput, calls=%fused_computation.12.clone.1 | convolution fusion | flops 805306368 | bytes 6291456 | tf_op jit(solution)/shard_map/while/body/eval_jaxpr/ptu,puv->ptv/dot_general | solution.py:83
  162.2 6.2 %fusion.69 = f32[32,128,128]{2,0,1:T(8,128)S(1)} fusion(s32[32]{0:T(128)S(1)} %get-tuple-element.157, f32[8,8,128,128]{3,2,1,0:T(8,128)} %bitcast.125), kind=kOutput, calls=%fused_computation.3.clone.1 | convolution fusion | flops 402655232 | bytes 6291584 | tf_op jit(solution)/shard_map/while/body/eval_jaxpr/dot_general | solution.py:21
  168.4 3.3 %fusion.67 = f32[32,128,128]{2,0,1:T(8,128)S(1)} fusion(s32[32]{0:T(128)S(1)} %fusion.66, f32[6,8,128,128]{3,2,1,0:T(8,128)S(1)} %bitcast.126), kind=kOutput, calls=%fused_computation.7.clone.1 | convolution fusion | flops 301991424 | bytes 5243008 | tf_op jit(solution)/shard_map/while/body/eval_jaxpr/dot_general | solution.py:21
  171.8 4.6 %fusion.70 = f32[32,128,128]{2,1,0:T(8,128)S(1)} fusion(f32[32,128,128]{2,0,1:T(8,128)S(1)} %fusion.67, f32[32,128,128]{2,0,1:T(8,128)S(1)} %fusion.69), kind=kOutput, calls=%fused_computation.12.clone.1 | convolution fusion | flops 805306368 | bytes 6291456 | tf_op jit(solution)/shard_map/while/body/eval_jaxpr/ptu,puv->ptv/dot_general | solution.py:83
  176.4 2.8 fusion.71
  179.2 6.2 %fusion.69 = f32[32,128,128]{2,0,1:T(8,128)S(1)} fusion(s32[32]{0:T(128)S(1)} %get-tuple-element.157, f32[8,8,128,128]{3,2,1,0:T(8,128)} %bitcast.125), kind=kOutput, calls=%fused_computation.3.clone.1 | convolution fusion | flops 402655232 | bytes 6291584 | tf_op jit(solution)/shard_map/while/body/eval_jaxpr/dot_general | solution.py:21
  185.4 3.3 %fusion.67 = f32[32,128,128]{2,0,1:T(8,128)S(1)} fusion(s32[32]{0:T(128)S(1)} %fusion.66, f32[6,8,128,128]{3,2,1,0:T(8,128)S(1)} %bitcast.126), kind=kOutput, calls=%fused_computation.7.clone.1 | convolution fusion | flops 301991424 | bytes 5243008 | tf_op jit(solution)/shard_map/while/body/eval_jaxpr/dot_general | solution.py:21
  188.7 4.6 %fusion.70 = f32[32,128,128]{2,1,0:T(8,128)S(1)} fusion(f32[32,128,128]{2,0,1:T(8,128)S(1)} %fusion.67, f32[32,128,128]{2,0,1:T(8,128)S(1)} %fusion.69), kind=kOutput, calls=%fused_computation.12.clone.1 | convolution fusion | flops 805306368 | bytes 6291456 | tf_op jit(solution)/shard_map/while/body/eval_jaxpr/ptu,puv->ptv/dot_general | solution.py:83
  193.3 2.8 fusion.71
  196.1 6.2 %fusion.69 = f32[32,128,128]{2,0,1:T(8,128)S(1)} fusion(s32[32]{0:T(128)S(1)} %get-tuple-element.157, f32[8,8,128,128]{3,2,1,0:T(8,128)} %bitcast.125), kind=kOutput, calls=%fused_computation.3.clone.1 | convolution fusion | flops 402655232 | bytes 6291584 | tf_op jit(solution)/shard_map/while/body/eval_jaxpr/dot_general | solution.py:21
  202.3 3.3 %fusion.67 = f32[32,128,128]{2,0,1:T(8,128)S(1)} fusion(s32[32]{0:T(128)S(1)} %fusion.66, f32[6,8,128,128]{3,2,1,0:T(8,128)S(1)} %bitcast.126), kind=kOutput, calls=%fused_computation.7.clone.1 | convolution fusion | flops 301991424 | bytes 5243008 | tf_op jit(solution)/shard_map/while/body/eval_jaxpr/dot_general | solution.py:21
  205.7 4.6 %fusion.70 = f32[32,128,128]{2,1,0:T(8,128)S(1)} fusion(f32[32,128,128]{2,0,1:T(8,128)S(1)} %fusion.67, f32[32,128,128]{2,0,1:T(8,128)S(1)} %fusion.69), kind=kOutput, calls=%fused_computation.12.clone.1 | convolution fusion | flops 805306368 | bytes 6291456 | tf_op jit(solution)/shard_map/while/body/eval_jaxpr/ptu,puv->ptv/dot_general | solution.py:83
  210.3 2.8 fusion.71
  213.0 53.5 %all_to_all.5 = f32[8,8,128,128]{3,1,2,0:T(8,128)} all-to-all(f32[8,8,128,128]{3,1,2,0:T(8,128)} %get-tuple-element.52), channel_id=1, replica_groups=mesh['rows'=8,'blk'=4] {'rows'}, dimensions={0} | all-to-all | bytes 8388608 | tf_op jit(solution)/shard_map/all_to_all | solution.py:90
  (102 shorter events, 29.8 us)
Async XLA Ops:
  6.5 1.1 copy-start
  6.5 4.6 %copy-start.3 = (s32[8,32]{1,0:T(8,128)S(1)}, s32[8,32]{1,0:T(8,128)}, u32[]{:S(2)}) copy-start(s32[8,32]{1,0:T(8,128)} %param.15) | copy-start | bytes 3076
  6.5 4.7 %copy-start.6 = (s32[8]{0:T(128)S(1)}, s32[8]{0:T(128)}, u32[]{:S(2)}) copy-start(s32[8]{0:T(128)} %param.17) | copy-start | bytes 100
  6.5 4.9 %copy-start.4 = (s32[8,32]{1,0:T(8,128)S(1)}, s32[8,32]{1,0:T(8,128)}, u32[]{:S(2)}) copy-start(s32[8,32]{1,0:T(8,128)} %param.16) | copy-start | bytes 3076
  6.5 5.0 %copy-start.5 = (s32[8,32]{1,0:T(8,128)S(1)}, s32[8,32]{1,0:T(8,128)}, u32[]{:S(2)}) copy-start(s32[8,32]{1,0:T(8,128)} %param.14) | copy-start | bytes 3076
  6.5 70.9 %all-gather.2.cloned.1.call-start = ((), (), s32[]{:S(2)}) async-start(), calls=%async_computation.1 | async-start | bytes 3932160 | tf_op jit(solution)/shard_map/all_gather | solution.py:76
  12.4 5.0 %collective-permute-start = (s32[4,1,32]{2,0,1:T(4,128)S(1)}, s32[4,1,32]{2,0,1:T(4,128)S(1)}, u32[]{:S(2)}, u32[]{:S(2)}) collective-permute-start(s32[4,1,32]{2,0,1:T(4,128)S(1)} %get-tuple-element.103), channel_id=1, source_target_pairs={{0,4},{4,0},{8,12},{12,8},{16,20},{20,16},{24,28},{28,24},{1,5},{5... | collective-permute-start | bytes 1544 | tf_op jit(solution)/shard_map/ppermute | solution.py:72
  13.0 7.1 %collective-permute-start.1 = (s32[4,1,32]{2,0,1:T(4,128)S(1)}, s32[4,1,32]{2,0,1:T(4,128)S(1)}, u32[]{:S(2)}, u32[]{:S(2)}) collective-permute-start(s32[4,1,32]{2,0,1:T(4,128)S(1)} %get-tuple-element.102), channel_id=1, source_target_pairs={{0,8},{4,12},{8,0},{12,4},{16,24},{20,28},{24,16},{28,20},{1,9},{5... | collective-permute-start | bytes 1544 | tf_op jit(solution)/shard_map/ppermute | solution.py:72
  15.5 4.7 %collective-permute-start.2 = (s32[4,1,32]{2,0,1:T(4,128)S(1)}, s32[4,1,32]{2,0,1:T(4,128)S(1)}, u32[]{:S(2)}, u32[]{:S(2)}) collective-permute-start(s32[4,1,32]{2,0,1:T(4,128)S(1)} %get-tuple-element.101), channel_id=1, source_target_pairs={{0,12},{4,8},{8,4},{12,0},{16,28},{20,24},{24,20},{28,16},{1,13},{... | collective-permute-start | bytes 1544 | tf_op jit(solution)/shard_map/ppermute | solution.py:72
  15.6 4.7 %collective-permute-start.3 = (s32[4,1,32]{2,0,1:T(4,128)S(1)}, s32[4,1,32]{2,0,1:T(4,128)S(1)}, u32[]{:S(2)}, u32[]{:S(2)}) collective-permute-start(s32[4,1,32]{2,0,1:T(4,128)S(1)} %get-tuple-element.100), channel_id=1, source_target_pairs={{0,16},{4,20},{8,24},{12,28},{16,0},{20,4},{24,8},{28,12},{1,17},{... | collective-permute-start | bytes 1544 | tf_op jit(solution)/shard_map/ppermute | solution.py:72
  17.3 3.0 %collective-permute-start.4 = (s32[4,1,32]{2,0,1:T(4,128)S(1)}, s32[4,1,32]{2,0,1:T(4,128)S(1)}, u32[]{:S(2)}, u32[]{:S(2)}) collective-permute-start(s32[4,1,32]{2,0,1:T(4,128)S(1)} %get-tuple-element.99), channel_id=1, source_target_pairs={{0,20},{4,16},{8,28},{12,24},{16,4},{20,0},{24,12},{28,8},{1,21},{... | collective-permute-start | bytes 1544 | tf_op jit(solution)/shard_map/ppermute | solution.py:72
  17.4 4.5 %collective-permute-start.5 = (s32[4,1,32]{2,0,1:T(4,128)S(1)}, s32[4,1,32]{2,0,1:T(4,128)S(1)}, u32[]{:S(2)}, u32[]{:S(2)}) collective-permute-start(s32[4,1,32]{2,0,1:T(4,128)S(1)} %get-tuple-element.98), channel_id=1, source_target_pairs={{0,24},{4,28},{8,16},{12,20},{16,8},{20,12},{24,0},{28,4},{1,25},{... | collective-permute-start | bytes 1544 | tf_op jit(solution)/shard_map/ppermute | solution.py:72
  20.1 3.9 %collective-permute-start.6 = (s32[4,1,32]{2,0,1:T(4,128)S(1)}, s32[4,1,32]{2,0,1:T(4,128)S(1)}, u32[]{:S(2)}, u32[]{:S(2)}) collective-permute-start(s32[4,1,32]{2,0,1:T(4,128)S(1)} %get-tuple-element.97), channel_id=1, source_target_pairs={{0,28},{4,24},{8,20},{12,16},{16,12},{20,8},{24,4},{28,0},{1,29},{... | collective-permute-start | bytes 1544 | tf_op jit(solution)/shard_map/ppermute | solution.py:72
  77.5 6.2 %copy-start.1 = (f32[48,128,128]{2,1,0:T(8,128)S(1)}, f32[48,128,128]{2,1,0:T(8,128)}, u32[]{:S(2)}) copy-start(f32[48,128,128]{2,1,0:T(8,128)} %get-tuple-element.184) | copy-start | bytes 9437188 | tf_op jit(solution)/shard_map/while
  94.4 6.2 %copy-start.1 = (f32[48,128,128]{2,1,0:T(8,128)S(1)}, f32[48,128,128]{2,1,0:T(8,128)}, u32[]{:S(2)}) copy-start(f32[48,128,128]{2,1,0:T(8,128)} %get-tuple-element.184) | copy-start | bytes 9437188 | tf_op jit(solution)/shard_map/while
  111.4 6.2 %copy-start.1 = (f32[48,128,128]{2,1,0:T(8,128)S(1)}, f32[48,128,128]{2,1,0:T(8,128)}, u32[]{:S(2)}) copy-start(f32[48,128,128]{2,1,0:T(8,128)} %get-tuple-element.184) | copy-start | bytes 9437188 | tf_op jit(solution)/shard_map/while
  128.3 6.2 %copy-start.1 = (f32[48,128,128]{2,1,0:T(8,128)S(1)}, f32[48,128,128]{2,1,0:T(8,128)}, u32[]{:S(2)}) copy-start(f32[48,128,128]{2,1,0:T(8,128)} %get-tuple-element.184) | copy-start | bytes 9437188 | tf_op jit(solution)/shard_map/while
  145.3 6.2 %copy-start.1 = (f32[48,128,128]{2,1,0:T(8,128)S(1)}, f32[48,128,128]{2,1,0:T(8,128)}, u32[]{:S(2)}) copy-start(f32[48,128,128]{2,1,0:T(8,128)} %get-tuple-element.184) | copy-start | bytes 9437188 | tf_op jit(solution)/shard_map/while
  162.2 6.2 %copy-start.1 = (f32[48,128,128]{2,1,0:T(8,128)S(1)}, f32[48,128,128]{2,1,0:T(8,128)}, u32[]{:S(2)}) copy-start(f32[48,128,128]{2,1,0:T(8,128)} %get-tuple-element.184) | copy-start | bytes 9437188 | tf_op jit(solution)/shard_map/while
  179.2 6.2 %copy-start.1 = (f32[48,128,128]{2,1,0:T(8,128)S(1)}, f32[48,128,128]{2,1,0:T(8,128)}, u32[]{:S(2)}) copy-start(f32[48,128,128]{2,1,0:T(8,128)} %get-tuple-element.184) | copy-start | bytes 9437188 | tf_op jit(solution)/shard_map/while
  196.1 6.2 %copy-start.1 = (f32[48,128,128]{2,1,0:T(8,128)S(1)}, f32[48,128,128]{2,1,0:T(8,128)}, u32[]{:S(2)}) copy-start(f32[48,128,128]{2,1,0:T(8,128)} %get-tuple-element.184) | copy-start | bytes 9437188 | tf_op jit(solution)/shard_map/while
  266.6 2.5 copy-start.2
Sparse Core Ops, SparseCore 0:
  11.3 66.1 all-gather.1
